TPU v7x, 32 devices: a whole 2x2x4 slice. The times are simulated.
32 devices in a mesh: doc: 8 (over y, x, core), seq: 4 (over z).
Axes of the slice: x: 2, y: 2, z: 4, core: 2. Of those that a mesh axis runs over, the one named last changes fastest.
Arguments:
- inputs: bfloat16 [16, 1024, 768], P('doc', 'seq'), may hold values from -6 to 6
- attn_gain: float32 [768], replicated, may hold values from 0.5 to 1.5
- qkv_weight: bfloat16 [768, 2304], replicated, may hold values from -0.25 to 0.25
- attn_out_weight: bfloat16 [768, 768], replicated, may hold values from -2 to 2
- mlp_gain: float32 [768], replicated, may hold values from 0.5 to 1.5
- mlp_in_weight: bfloat16 [768, 2304], replicated, may hold values from -0.21875 to 0.21875
- mlp_out_weight: bfloat16 [1152, 768], replicated, may hold values from -0.1875 to 0.1875
- cotangent: bfloat16 [16, 1024, 768], P('doc', 'seq'), may hold values from -6 to 6
Outputs:
- output: bfloat16 [16, 1024, 768], P('doc', 'seq')
- input_grad: bfloat16 [16, 1024, 768], P('doc', 'seq')
- attn_gain_grad: float32 [768], replicated
- qkv_weight_grad: float32 [768, 2304], replicated
- attn_out_weight_grad: float32 [768, 768], replicated
- mlp_gain_grad: float32 [768], replicated
- mlp_in_weight_grad: float32 [768, 2304], replicated
- mlp_out_weight_grad: float32 [1152, 768], replicated
All inputs are finite; a program needn't handle non-finite values.
Results may differ from a plain program's by a relative error of at most 0.015.
Values may be sent and summed in bfloat16 or wider, within the bound.
A program may use at most 128 MiB of HBM per device.

v0:
```python
import jax
import jax.numpy as jnp
from jax import lax
from jax.sharding import PartitionSpec as P

HEAD_DIM = 64
ROPE_THETA = 160000.0
NORM_EPSILON = 1e-05


def norm_rows(values, scale_gain):
    row_mean = jnp.mean(values, axis=-1, keepdims=True)
    centered = values - row_mean
    variance = jnp.mean(centered * centered, axis=-1, keepdims=True)
    return centered * lax.rsqrt(variance + NORM_EPSILON) * scale_gain


def rotary_tables(positions, head_width):
    half_width = head_width // 2
    frequency = ROPE_THETA ** (-(jnp.arange(half_width, dtype=jnp.float32) * 2.0) / head_width)
    angles = positions.astype(jnp.float32)[:, None] * frequency[None, :]
    angles = jnp.concatenate([angles, angles], axis=-1)
    return (jnp.cos(angles)[:, None, :], jnp.sin(angles)[:, None, :])


def rotate(values, cosine_table, sine_table):
    half_width = values.shape[-1] // 2
    turned = jnp.concatenate([-values[..., half_width:], values[..., :half_width]], axis=-1)
    return values * cosine_table + turned * sine_table


def rotate_back(gradient, cosine_table, sine_table):
    half_width = gradient.shape[-1] // 2
    sined = gradient * sine_table
    turned = jnp.concatenate([sined[..., half_width:], -sined[..., :half_width]], axis=-1)
    return gradient * cosine_table + turned


def gelu_product(gate_up):
    half_width = gate_up.shape[-1] // 2
    return jax.nn.gelu(gate_up[..., :half_width], approximate=False) * gate_up[..., half_width:]


def split_heads(columns):
    return columns.reshape(columns.shape[0], columns.shape[1] // HEAD_DIM, HEAD_DIM)


def attend_forward(queries, key_rows, value_rows):
    length, features = queries.shape
    scores = (
        jnp.einsum(
            "qhd,khd->hqk",
            split_heads(queries),
            split_heads(key_rows),
            preferred_element_type=jnp.float32,
        )
        * 0.125
    )
    row_max = jnp.max(scores, axis=-1, keepdims=True)
    exp_scores = jnp.exp(scores - row_max)
    row_total = jnp.sum(exp_scores, axis=-1, keepdims=True)
    softmax_low = (exp_scores / row_total).astype(jnp.bfloat16)
    mixed_rows = jnp.einsum(
        "hqk,khd->qhd", softmax_low, split_heads(value_rows), preferred_element_type=jnp.float32
    )
    return (
        mixed_rows.reshape(length, features).astype(jnp.bfloat16),
        (row_max + jnp.log(row_total))[..., 0],
    )


def attend_backward(queries, key_rows, value_rows, grad_mixed, log_total, cosine_table, sine_table):
    length, features = queries.shape
    query_heads = split_heads(queries)
    key_heads = split_heads(key_rows)
    value_heads = split_heads(value_rows)
    grad_heads = split_heads(grad_mixed)
    scores = (
        jnp.einsum("qhd,khd->hqk", query_heads, key_heads, preferred_element_type=jnp.float32)
        * 0.125
    )
    softmax_out = jnp.exp(scores - log_total[..., None])
    grad_soft = jnp.einsum(
        "qhd,khd->hqk", grad_heads, value_heads, preferred_element_type=jnp.float32
    )
    row_inner = jnp.sum(softmax_out * grad_soft, axis=-1, keepdims=True)
    grad_scores = (softmax_out * (grad_soft - row_inner)).astype(jnp.bfloat16)
    grad_query = (
        jnp.einsum("hqk,khd->qhd", grad_scores, key_heads, preferred_element_type=jnp.float32)
        * 0.125
    )
    grad_key = (
        jnp.einsum("hqk,qhd->khd", grad_scores, query_heads, preferred_element_type=jnp.float32)
        * 0.125
    )
    grad_value = jnp.einsum(
        "hqk,qhd->khd",
        softmax_out.astype(jnp.bfloat16),
        grad_heads,
        preferred_element_type=jnp.float32,
    )
    grad_query = (
        rotate_back(grad_query, cosine_table, sine_table)
        .reshape(length, features)
        .astype(jnp.bfloat16)
    )
    grad_key = (
        rotate_back(grad_key, cosine_table, sine_table)
        .reshape(length, features)
        .astype(jnp.bfloat16)
    )
    return (grad_query, grad_key, grad_value.reshape(length, features).astype(jnp.bfloat16))


def per_device(
    inputs,
    attn_gain,
    qkv_weight,
    attn_out_weight,
    mlp_gain,
    mlp_in_weight,
    mlp_out_weight,
    cotangent,
):
    doc_count, row_count, features = inputs.shape
    token_count = doc_count * row_count
    length = row_count * lax.axis_size("seq")
    flat_in = inputs.reshape(token_count, features).astype(jnp.float32)
    normed = norm_rows(flat_in, attn_gain).astype(jnp.bfloat16)
    projected = jnp.dot(normed, qkv_weight, preferred_element_type=jnp.float32)
    projected = projected.reshape(doc_count, row_count, 3 * features)
    local_cos, local_sin = rotary_tables(
        lax.axis_index("seq") * row_count + jnp.arange(row_count, dtype=jnp.int32), HEAD_DIM
    )

    def turned_low(columns):
        shaped = columns.reshape(doc_count, row_count, features // HEAD_DIM, HEAD_DIM)
        return (
            rotate(shaped, local_cos, local_sin)
            .reshape(doc_count, row_count, features)
            .astype(jnp.bfloat16)
        )

    queries = turned_low(projected[..., :features])
    key_rows = turned_low(projected[..., features : 2 * features])
    value_rows = projected[..., 2 * features :].astype(jnp.bfloat16)
    head_queries, head_keys, head_values = (
        lax.all_to_all(queries, "seq", split_axis=2, concat_axis=1, tiled=True),
        lax.all_to_all(key_rows, "seq", split_axis=2, concat_axis=1, tiled=True),
        lax.all_to_all(value_rows, "seq", split_axis=2, concat_axis=1, tiled=True),
    )
    mixed_heads, log_total = lax.map(
        lambda bundle: attend_forward(*bundle), (head_queries, head_keys, head_values)
    )
    attended = lax.all_to_all(mixed_heads, "seq", split_axis=1, concat_axis=2, tiled=True).reshape(
        token_count, features
    )
    hidden_res = flat_in + jnp.dot(attended, attn_out_weight, preferred_element_type=jnp.float32)
    normed_two = norm_rows(hidden_res, mlp_gain).astype(jnp.bfloat16)
    gate_up = jnp.dot(normed_two, mlp_in_weight, preferred_element_type=jnp.float32)
    inner_act, inner_pull = jax.vjp(gelu_product, gate_up)
    inner_act = inner_act.astype(jnp.bfloat16)
    result = hidden_res + jnp.dot(inner_act, mlp_out_weight, preferred_element_type=jnp.float32)
    output = result.astype(jnp.bfloat16).reshape(doc_count, row_count, features)
    upstream = cotangent.reshape(token_count, features)
    grad_mlp_out = jnp.einsum("tf,td->fd", inner_act, upstream, preferred_element_type=jnp.float32)
    grad_inner = jnp.einsum(
        "td,fd->tf", upstream, mlp_out_weight, preferred_element_type=jnp.float32
    )
    grad_gate_up = inner_pull(grad_inner)[0].astype(jnp.bfloat16)
    grad_mlp_in = jnp.einsum(
        "td,tf->df", normed_two, grad_gate_up, preferred_element_type=jnp.float32
    )
    grad_normed_two = jnp.einsum(
        "tf,df->td", grad_gate_up, mlp_in_weight, preferred_element_type=jnp.float32
    )
    _, second_pull = jax.vjp(norm_rows, hidden_res, mlp_gain)
    grad_hidden, grad_mlp_gain = second_pull(grad_normed_two)
    grad_hidden = grad_hidden + upstream.astype(jnp.float32)
    grad_branch = grad_hidden.astype(jnp.bfloat16)
    grad_attn_out = jnp.einsum(
        "td,te->de", attended, grad_branch, preferred_element_type=jnp.float32
    )
    grad_attended = jnp.einsum(
        "te,de->td", grad_branch, attn_out_weight, preferred_element_type=jnp.float32
    )
    grad_attended = grad_attended.astype(jnp.bfloat16).reshape(doc_count, row_count, features)
    grad_mixed = lax.all_to_all(grad_attended, "seq", split_axis=2, concat_axis=1, tiled=True)
    full_cos, full_sin = rotary_tables(jnp.arange(length, dtype=jnp.int32), HEAD_DIM)
    grad_head_q, grad_head_k, grad_head_v = lax.map(
        lambda bundle: attend_backward(*bundle, full_cos, full_sin),
        (head_queries, head_keys, head_values, grad_mixed, log_total),
    )
    grad_tok_q, grad_tok_k, grad_tok_v = (
        lax.all_to_all(grad_head_q, "seq", split_axis=1, concat_axis=2, tiled=True),
        lax.all_to_all(grad_head_k, "seq", split_axis=1, concat_axis=2, tiled=True),
        lax.all_to_all(grad_head_v, "seq", split_axis=1, concat_axis=2, tiled=True),
    )
    grad_tok_q = grad_tok_q.reshape(token_count, features)
    grad_tok_k = grad_tok_k.reshape(token_count, features)
    grad_tok_v = grad_tok_v.reshape(token_count, features)
    grad_qkv = jnp.concatenate(
        [
            jnp.einsum("td,te->de", normed, grad_tok_q, preferred_element_type=jnp.float32),
            jnp.einsum("td,te->de", normed, grad_tok_k, preferred_element_type=jnp.float32),
            jnp.einsum("td,te->de", normed, grad_tok_v, preferred_element_type=jnp.float32),
        ],
        axis=1,
    )
    grad_normed = jnp.einsum(
        "te,de->td", grad_tok_q, qkv_weight[:, :features], preferred_element_type=jnp.float32
    )
    grad_normed = grad_normed + jnp.einsum(
        "te,de->td",
        grad_tok_k,
        qkv_weight[:, features : 2 * features],
        preferred_element_type=jnp.float32,
    )
    grad_normed = grad_normed + jnp.einsum(
        "te,de->td", grad_tok_v, qkv_weight[:, 2 * features :], preferred_element_type=jnp.float32
    )
    _, first_pull = jax.vjp(norm_rows, flat_in, attn_gain)
    grad_input, grad_attn_gain = first_pull(grad_normed)
    grad_input = (
        (grad_input + grad_hidden).astype(jnp.bfloat16).reshape(doc_count, row_count, features)
    )
    summed = lax.psum(
        (grad_attn_gain, grad_qkv, grad_attn_out, grad_mlp_gain, grad_mlp_in, grad_mlp_out),
        ("doc", "seq"),
    )
    return (output, grad_input, summed[0], summed[1], summed[2], summed[3], summed[4], summed[5])


def solution(mesh):
    placed = (P("doc", "seq", None), P(), P(), P(), P(), P(), P(), P("doc", "seq", None))
    return jax.shard_map(
        per_device,
        mesh=mesh,
        in_specs=placed,
        out_specs=(P("doc", "seq", None), P("doc", "seq", None), P(), P(), P(), P(), P(), P()),
        check_vma=False,
    )
```

profile of v0, /device:TPU:0, one launch (start us, length us, event | category | flops | bytes accessed | tf_op | source)
XLA Modules:
  0.0 743.3 jit_solution(14533819958164597936)
XLA Ops:
  12.8 4.3 fusion.13
  20.2 3.0 copy.71
  23.3 6.3 all-to-all-start
  29.6 3.9 fusion.58
  33.5 3.0 copy.81
  39.2 3.0 copy.82
  50.4 3.0 copy.75
  56.1 3.0 copy.77
  59.2 5.0 add_convert_fusion.3
  64.1 3.0 copy.78
  67.2 5.1 all-to-all-start.1
  72.3 3.0 copy.83
  75.3 16.6 %all-to-all-done.1 = bf16[2,256,768]{1,0,2:T(2,128)(2,1)} async-done(((bf16[2,256,768]{1,0,2:T(2,128)(2,1)}), bf16[2,256,768]{1,0,2:T(2,128)(2,1)}, u32[]{:S(2)}, u32[]{:S(2)}) %all-to-all-start.1) | async-done | bytes 786464 | tf_op jit(solution)/shard_map/all_to_all | solution.py:148
  91.9 4.4 all-to-all-start.2
  100.8 15.2 %all-to-all-done.2 = bf16[2,256,768]{1,0,2:T(2,128)(2,1)} async-done(((bf16[2,256,768]{1,0,2:T(2,128)(2,1)}), bf16[2,256,768]{1,0,2:T(2,128)(2,1)}, u32[]{:S(2)}, u32[]{:S(2)}) %all-to-all-start.2) | async-done | bytes 786464 | tf_op jit(solution)/shard_map/all_to_all | solution.py:149
  119.2 19.5 %while.26 = (s32[]{:T(128)}, bf16[2,1024,192]{1,2,0:T(8,128)(2,1)}, f32[2,3,1024]{2,1,0:T(4,128)}, bf16[2,1024,192]{1,2,0:T(8,128)(2,1)}, bf16[2,1024,192]{1,2,0...) while((s32[]{:T(128)}, bf16[2,1024,192]{1,2,0:T(8,128)(2,1)}, f32[2,3,1024]{2,1,0:T(4,128)}, ...), condition=%wide.region_5.6_spmd, body=%wide.region_2.5_spmd.sunk | while | flops 833811456 | bytes 48861340 | solution.py:152
  138.7 3.6 copy.86
  142.3 29.5 %all_to_all.132 = bf16[2,1024,192]{2,0,1:T(2,128)(2,1)} all-to-all(bf16[2,1024,192]{2,0,1:T(2,128)(2,1)} %copy.86), channel_id=1, replica_groups=mesh['doc'=8,'seq'=4] {'seq'}, dimensions={1} | all-to-all | bytes 1572864 | tf_op jit(solution)/shard_map/all_to_all | solution.py:155
  171.8 5.9 copy.87
  184.3 5.6 fusion.39
  200.5 3.5 all-to-all-start.4
  205.8 17.4 %all-to-all-done.4 = bf16[2,256,768]{1,0,2:T(2,128)(2,1)S(1)} async-done(((bf16[2,256,768]{1,0,2:T(2,128)(2,1)}), bf16[2,256,768]{1,0,2:T(2,128)(2,1)S(1)}, u32[]{:S(2)}, u32[]{:S(2)}) %all-to-all-start.4) | async-done | bytes 786464 | tf_op jit(solution)/shard_map/all_to_all | solution.py:188
  227.2 60.3 %while.27 = (s32[]{:T(128)}, bf16[2,1024,192]{1,2,0:T(8,128)(2,1)}, bf16[2,1024,192]{1,2,0:T(8,128)(2,1)}, bf16[2,1024,192]{1,2,0:T(8,128)(2,1)}, bf16[2,1024,19...) while((s32[]{:T(128)}, bf16[2,1024,192]{1,2,0:T(8,128)(2,1)}, ...), condition=%wide.region_12.13_spmd, body=%wide.region_10.12_spmd.sunk | while | flops 2053501952 | bytes 154489168 | solution.py:190
  238.6 3.7 multiply_reduce_fusion.8
  242.3 5.3 multiply_convert_fusion.6
  247.6 4.1 convolution_bitcast_fusion.3
  268.8 3.7 multiply_reduce_fusion.8
  272.5 5.3 multiply_convert_fusion.6
  277.8 4.1 convolution_bitcast_fusion.3
  287.5 3.7 copy.95
  291.2 3.5 all-to-all-start.7
  296.8 23.1 %all-to-all-done.7 = bf16[2,1024,192]{2,0,1:T(2,128)(2,1)S(1)} async-done(((bf16[2,1024,192]{2,0,1:T(2,128)(2,1)}), bf16[2,1024,192]{2,0,1:T(2,128)(2,1)S(1)}, u32[]{:S(2)}, u32[]{:S(2)}) %all-to-all-start.7) | async-done | bytes 786464 | tf_op jit(solution)/shard_map/all_to_all | solution.py:197
  319.9 3.5 all-to-all-start.5
  325.5 23.1 %all-to-all-done.5 = bf16[2,1024,192]{2,0,1:T(2,128)(2,1)S(1)} async-done(((bf16[2,1024,192]{2,0,1:T(2,128)(2,1)}), bf16[2,1024,192]{2,0,1:T(2,128)(2,1)S(1)}, u32[]{:S(2)}, u32[]{:S(2)}) %all-to-all-start.5) | async-done | bytes 786464 | tf_op jit(solution)/shard_map/all_to_all | solution.py:195
  348.6 4.2 all-to-all-start.6
  353.1 3.6 fusion.61
  356.8 2.9 fusion.62
  360.9 5.2 fusion.40
  366.1 4.7 copy.96
  371.9 5.7 copy.92
  379.8 5.7 copy.94
  391.0 3.2 pad_maximum_fusion
  394.9 4.0 add_convert_fusion.2
  403.7 43.1 %all-reduce.2 = (f32[768]{0:T(1024)}, f32[768]{0:T(1024)}) all-reduce(f32[768]{0:T(1024)S(1)} %get-tuple-element.139, f32[768]{0:T(1024)S(1)} %copy-done.49), channel_id=1, replica_groups=mesh['doc'=8,'seq'=4] {'doc','seq'}, use_global_device_ids=true, to_apply=%region_16.17 | all-reduce | flops 1536 | bytes 12288 | tf_op jit(solution)/shard_map/psum | solution.py:227
  446.8 3.0 add_convert_fusion.1
  449.8 268.4 %all-reduce.6.cloned.1.call-done = (f32[768,2304]{0,1:T(8,128)}, f32[768,768]{1,0:T(8,128)}, f32[768,2304]{1,0:T(8,128)}, f32[1152,768]{1,0:T(8,128)}) async-done(((f32[768,2304]{0,1:T(8,128)}, f32[768,768]{1,0:T(8,128)}, f32[768,2304]{1,0:T(8,128)}, f32[1152,768]{1,0:T(8,128)}), (f32[768,2304]{0,1:T(8,128)}, f32[768,768]{1,0:T(8,128)}, f32[768,2304]{1,0:T(8,128)}, ...) | async-done | bytes 20054032 | tf_op jit(solution)/shard_map/psum | solution.py:227
  718.3 8.1 %copy.97 = f32[768,2304]{1,0:T(8,128)} copy(f32[768,2304]{0,1:T(8,128)} %get-tuple-element.177) | data formatting | bytes 14155776
  727.8 6.6 copy.145
  (236 shorter events, 128.8 us)
Async XLA Ops:
  7.2 174.9 %copy-start = (bf16[768,2304]{1,0:T(8,128)(2,1)S(1)}, bf16[768,2304]{1,0:T(8,128)(2,1)}, u32[]{:S(2)}) copy-start(bf16[768,2304]{1,0:T(8,128)(2,1)} %param.17) | copy-start | bytes 10616836
  12.8 4.3 copy-start.8
  17.1 2.2 copy-start.10
  23.3 43.9 %all-to-all-start = ((bf16[2,256,768]{1,0,2:T(2,128)(2,1)}), bf16[2,256,768]{1,0,2:T(2,128)(2,1)}, u32[]{:S(2)}, u32[]{:S(2)}) async-start(bf16[2,256,768]{1,0,2:T(2,128)(2,1)} %copy.71), calls=%async_computation | async-start | bytes 1572864 | tf_op jit(solution)/shard_map/all_to_all | solution.py:150
  33.5 8.8 %copy-start.50 = (f32[32]{0:T(128)}, f32[32]{0:T(128)S(1)}, u32[]{:S(2)}) copy-start(f32[32]{0:T(128)S(1)} %multiply_power_fusion) | copy-start | bytes 388
  67.2 24.7 %all-to-all-start.1 = ((bf16[2,256,768]{1,0,2:T(2,128)(2,1)}), bf16[2,256,768]{1,0,2:T(2,128)(2,1)}, u32[]{:S(2)}, u32[]{:S(2)}) async-start(bf16[2,256,768]{1,0,2:T(2,128)(2,1)} %copy.78), calls=%async_computation.1 | async-start | bytes 1572864 | tf_op jit(solution)/shard_map/all_to_all | solution.py:148
  91.9 24.0 %all-to-all-start.2 = ((bf16[2,256,768]{1,0,2:T(2,128)(2,1)}), bf16[2,256,768]{1,0,2:T(2,128)(2,1)}, u32[]{:S(2)}, u32[]{:S(2)}) async-start(bf16[2,256,768]{1,0,2:T(2,128)(2,1)} %copy.83), calls=%async_computation.2 | async-start | bytes 1572864 | tf_op jit(solution)/shard_map/all_to_all | solution.py:149
  125.3 2.7 copy-start.26
  135.1 2.7 copy-start.26
  179.0 3.0 copy-start.28
  179.1 3.1 copy-start.38
  181.7 13.2 %copy-start.6 = (f32[512,768]{1,0:T(8,128)}, f32[512,768]{1,0:T(8,128)S(1)}, u32[]{:S(2)}) copy-start(f32[512,768]{1,0:T(8,128)S(1)} %get-tuple-element.225) | copy-start | bytes 4718596
  181.8 13.2 %copy-start.41 = (f32[512]{0:T(512)}, f32[512]{0:T(512)S(1)}, u32[]{:S(2)}) copy-start(f32[512]{0:T(512)S(1)} %broadcast_multiply_fusion.3) | copy-start | bytes 6148
  182.1 12.8 %copy-start.43 = (f32[512]{0:T(512)}, f32[512]{0:T(512)S(1)}, u32[]{:S(2)}) copy-start(f32[512]{0:T(512)S(1)} %fusion.46) | copy-start | bytes 6148
  182.1 2.1 copy-start.13
  182.1 2.1 copy-start.52
  189.9 2.2 copy-start.35
  192.1 2.8 copy-start.11
  196.0 2.7 copy-start.5
  197.9 2.6 copy-start.33
  198.7 5.3 copy-start.51
  200.5 22.6 %all-to-all-start.4 = ((bf16[2,256,768]{1,0,2:T(2,128)(2,1)}), bf16[2,256,768]{1,0,2:T(2,128)(2,1)S(1)}, u32[]{:S(2)}, u32[]{:S(2)}) async-start(bf16[2,256,768]{1,0,2:T(2,128)(2,1)} %copy.88), calls=%async_computation.4 | async-start | bytes 1572864 | tf_op jit(solution)/shard_map/all_to_all | solution.py:188
  247.6 4.6 copy-start.2
  277.8 4.6 copy-start.2
  287.5 7.2 copy-start.22
  291.2 28.7 %all-to-all-start.7 = ((bf16[2,1024,192]{2,0,1:T(2,128)(2,1)}), bf16[2,1024,192]{2,0,1:T(2,128)(2,1)S(1)}, u32[]{:S(2)}, u32[]{:S(2)}) async-start(bf16[2,1024,192]{2,0,1:T(2,128)(2,1)} %copy.95), calls=%async_computation.7 | async-start | bytes 2097152 | tf_op jit(solution)/shard_map/all_to_all | solution.py:197
  294.7 28.7 %copy-start.25 = (bf16[2,1024,192]{1,2,0:T(8,128)(2,1)S(1)}, bf16[2,1024,192]{1,2,0:T(8,128)(2,1)}, u32[]{:S(2)}) copy-start(bf16[2,1024,192]{1,2,0:T(8,128)(2,1)} %get-tuple-element.103) | copy-start | bytes 2359300
  319.9 28.7 %copy-start.17 = (bf16[2,1024,192]{2,0,1:T(2,128)(2,1)}, bf16[2,1024,192]{2,0,1:T(2,128)(2,1)S(1)}, u32[]{:S(2)}) copy-start(bf16[2,1024,192]{2,0,1:T(2,128)(2,1)S(1)} %all-to-all-done.7) | copy-start | bytes 2359300
  319.9 28.7 %all-to-all-start.5 = ((bf16[2,1024,192]{2,0,1:T(2,128)(2,1)}), bf16[2,1024,192]{2,0,1:T(2,128)(2,1)S(1)}, u32[]{:S(2)}, u32[]{:S(2)}) async-start(bf16[2,1024,192]{2,0,1:T(2,128)(2,1)} %copy.91), calls=%async_computation.5 | async-start | bytes 2097152 | tf_op jit(solution)/shard_map/all_to_all | solution.py:195
  348.6 8.1 %copy-start.18 = (bf16[2,1024,192]{2,0,1:T(2,128)(2,1)}, bf16[2,1024,192]{2,0,1:T(2,128)(2,1)S(1)}, u32[]{:S(2)}) copy-start(bf16[2,1024,192]{2,0,1:T(2,128)(2,1)S(1)} %all-to-all-done.5) | copy-start | bytes 2359300
  348.6 31.2 %all-to-all-start.6 = ((bf16[2,1024,192]{2,0,1:T(2,128)(2,1)}), bf16[2,1024,192]{2,0,1:T(2,128)(2,1)}, u32[]{:S(2)}, u32[]{:S(2)}) async-start(bf16[2,1024,192]{2,0,1:T(2,128)(2,1)} %copy.93), calls=%async_computation.6 | async-start | bytes 2097152 | tf_op jit(solution)/shard_map/all_to_all | solution.py:196
  352.9 3.9 copy-start.14
  352.9 365.4 %all-reduce.6.cloned.1.call-start = ((), (), s32[]{:S(2)}) async-start(), calls=%async_computation.8 | async-start | bytes 40108032 | tf_op jit(solution)/shard_map/psum | solution.py:227
  353.1 3.7 copy-start.16
  356.8 3.0 copy-start.7
  356.8 3.0 copy-start.12
  356.8 4.1 copy-start.36
  356.8 4.1 copy-start.39
  356.8 4.1 copy-start.42
  356.8 4.1 copy-start.44
  377.6 9.3 %copy-start.9 = (bf16[2,256,768]{2,1,0:T(8,128)(2,1)S(1)}, bf16[2,256,768]{2,1,0:T(8,128)(2,1)}, u32[]{:S(2)}) copy-start(bf16[2,256,768]{2,1,0:T(8,128)(2,1)} %copy-done.8) | copy-start | bytes 2359300
  386.8 3.0 copy-start.31
  394.9 4.1 copy-start.30
  394.9 4.1 copy-start.37
  402.9 44.0 %copy-start.46 = (f32[512]{0:T(512)S(1)}, f32[512]{0:T(512)}, u32[]{:S(2)}) copy-start(f32[512]{0:T(512)} %copy-done.45) | copy-start | bytes 6148
  718.3 8.1 %copy-start.34 = (f32[768,768]{1,0:T(8,128)S(1)}, f32[768,768]{1,0:T(8,128)}, u32[]{:S(2)}) copy-start(f32[768,768]{1,0:T(8,128)} %get-tuple-element.433) | copy-start | bytes 7077892
  727.8 6.6 copy-start.19
  727.8 8.4 %copy-start.1 = (bf16[768,2304]{1,0:T(8,128)(2,1)S(1)}, bf16[768,2304]{1,0:T(8,128)(2,1)}, u32[]{:S(2)}) copy-start(bf16[768,2304]{1,0:T(8,128)(2,1)} %param.17) | copy-start | bytes 10616836
  (22 other events, 23.3 us)
Sparse Core Ops, SparseCore 0:
  394.3 323.9 all-reduce.5
where the time goes:
time: 752 us; the launch traced here: 743 us
  waiting for transfers between devices  364 us (48%)
  local copies, waits for them, and re-layouts  133 us (18%)
  matrix products  77.8 us (10%)
  blocking collectives  72.7 us (10%)
  other arithmetic  49.8 us (7%)
  starting transfers between devices  30.8 us (4%)
  between operations  14.9 us (2%)
    psum x1, waiting for transfers between devices, per_device(): lax.psum((grad_attn_gain, grad_qkv, grad_attn_out, grad_mlp_gain, grad_ml...  268 us
    psum x1, blocking collectives, per_device(): lax.psum((grad_attn_gain, grad_qkv, grad_attn_out, grad_mlp_gain, grad_ml...  43.1 us
    unnamed x102, local copies, waits for them, and re-layouts  30.9 us
    all_to_all x1, blocking collectives, per_device(): lax.all_to_all(mixed_heads, 'seq', split_axis=1, concat_axis=2, tiled=True)  29.5 us
    all_to_all x1, waiting for transfers between devices, per_device(): lax.all_to_all(grad_head_v, 'seq', split_axis=1, concat_axis=2, tiled=True)  23.1 us
    all_to_all x1, waiting for transfers between devices, per_device(): lax.all_to_all(grad_head_q, 'seq', split_axis=1, concat_axis=2, tiled=True)  23.1 us
    all_to_all x1, waiting for transfers between devices, per_device(): lax.all_to_all(grad_attended, 'seq', split_axis=2, concat_axis=1, tiled=T...  17.4 us
    all_to_all x1, waiting for transfers between devices, per_device(): lax.all_to_all(queries, 'seq', split_axis=2, concat_axis=1, tiled=True)  16.6 us
  transfers between devices with their start and end apart: 8, of which 6 were waited for; matrix products, arithmetic and copies ran while one was open for 12% of the time, Pallas kernels for 0%

commit v1 on v0

--- a/solution.py
+++ b/solution.py
@@ -1,3 +1,4 @@
+import functools
 import jax
 import jax.numpy as jnp
 from jax import lax
@@ -6,6 +7,38 @@
 HEAD_DIM = 64
 ROPE_THETA = 160000.0
 NORM_EPSILON = 1e-05
+
+
+def _arrange_kinds(vec, out_dim, z):
+    carry = vec.shape
+    near = vec.reshape(*carry[:out_dim], z, carry[out_dim] // z, *carry[out_dim + 1 :])
+    return jnp.moveaxis(near, out_dim, 0)
+
+
+def detail_the_seats_all(my_data, axis_k):
+    raw_out = list(my_data.shape[1:])
+    raw_out[axis_k] *= my_data.shape[0]
+    return jnp.moveaxis(my_data, 0, axis_k).reshape(raw_out)
+
+
+def review_the_levels_all(work_x, mesh_name, local, body):
+    tile_out, state_next = (lax.axis_size(mesh_name), lax.axis_index(mesh_name))
+    after = _arrange_kinds(work_x, local, tile_out)
+    by_rank = [after[state_next]]
+    dd = 1
+    while dd < tile_out:
+        tmp = after[state_next ^ dd]
+        small = lax.ppermute(
+            tmp, axis_name=mesh_name, perm=[(pp, pp ^ dd) for pp in range(tile_out)]
+        )
+        by_rank.append(small)
+        dd = dd + 1
+    mid_arr = jnp.stack(by_rank, 0)
+    after = mid_arr[state_next ^ jnp.arange(tile_out)]
+    return detail_the_seats_all(after, body)
+
+
+deliver_the_ratios = functools.partial(review_the_levels_all, mesh_name="seq", local=2, body=1)
 
 
 def norm_rows(values, scale_gain):
@@ -145,7 +178,7 @@
     key_rows = turned_low(projected[..., features : 2 * features])
     value_rows = projected[..., 2 * features :].astype(jnp.bfloat16)
     head_queries, head_keys, head_values = (
-        lax.all_to_all(queries, "seq", split_axis=2, concat_axis=1, tiled=True),
+        deliver_the_ratios(queries),
         lax.all_to_all(key_rows, "seq", split_axis=2, concat_axis=1, tiled=True),
         lax.all_to_all(value_rows, "seq", split_axis=2, concat_axis=1, tiled=True),
     )

time: 752 us -> 754 us (level)
    ppermute x0 -> x3, waiting for transfers between devices: none -> 27.7 us  [review_the_levels_all(): lax.ppermute(tmp, axis_name=mesh_name, perm=[(pp, pp ^ dd) for pp in rang...]
    all_to_all x1 -> x0, waiting for transfers between devices: 16.6 us -> none  [per_device(): lax.all_to_all(queries, 'seq', split_axis=2, concat_axis=1, tiled=True)]
    all_to_all x1, waiting for transfers between devices: 15.2 us -> 0.01 us  [per_device(): lax.all_to_all(key_rows, 'seq', split_axis=2, concat_axis=1, tiled=True)]
  transfers between devices with their start and end apart: 8 -> 10, of which waited for: 6 -> 6; matrix products, arithmetic and copies ran while one was open for 12% -> 12% of each run, Pallas kernels for 0% -> 0%
where the time goes in v1:
time: 754 us; the launch traced here: 745 us
  waiting for transfers between devices  360 us (48%)
  local copies, waits for them, and re-layouts  137 us (18%)
  matrix products  77.7 us (10%)
  blocking collectives  72.7 us (10%)
  other arithmetic  52 us (7%)
  starting transfers between devices  31 us (4%)
  between operations  14.9 us (2%)
    psum x1, waiting for transfers between devices, per_device(): lax.psum((grad_attn_gain, grad_qkv, grad_attn_out, grad_mlp_gain, grad_ml...  268 us
    psum x1, blocking collectives, per_device(): lax.psum((grad_attn_gain, grad_qkv, grad_attn_out, grad_mlp_gain, grad_ml...  43.2 us
    unnamed x102, local copies, waits for them, and re-layouts  30.9 us
    all_to_all x1, blocking collectives, per_device(): lax.all_to_all(mixed_heads, 'seq', split_axis=1, concat_axis=2, tiled=True)  29.5 us
    ppermute x3, waiting for transfers between devices, review_the_levels_all(): lax.ppermute(tmp, axis_name=mesh_name, perm=[(pp, pp ^ dd) for pp in rang...  27.7 us
    all_to_all x1, waiting for transfers between devices, per_device(): lax.all_to_all(grad_head_v, 'seq', split_axis=1, concat_axis=2, tiled=True)  23.1 us
    all_to_all x1, waiting for transfers between devices, per_device(): lax.all_to_all(grad_head_q, 'seq', split_axis=1, concat_axis=2, tiled=True)  23.1 us
    all_to_all x1, waiting for transfers between devices, per_device(): lax.all_to_all(grad_attended, 'seq', split_axis=2, concat_axis=1, tiled=T...  17.4 us
  transfers between devices with their start and end apart: 10, of which 6 were waited for; matrix products, arithmetic and copies ran while one was open for 12% of the time, Pallas kernels for 0%

profile of v1, /device:TPU:0, one launch (start us, length us, event | category | flops | bytes accessed | tf_op | source)
XLA Modules:
  0.0 745.4 jit_solution(16190331889369114551)
XLA Ops:
  12.8 4.3 fusion.13
  20.2 3.0 copy.70
  23.3 6.3 all-to-all-start
  29.6 3.9 fusion.59
  33.5 3.0 copy.79
  39.2 3.0 copy.80
  50.4 3.0 copy.74
  56.2 3.0 copy.76
  59.2 5.0 add_convert_fusion.3
  64.2 3.0 copy.81
  67.2 5.3 all-to-all-start.1
  76.9 3.8 collective-permute-start.2
  81.3 13.7 %collective-permute-done.2 = bf16[2,256,192]{1,2,0:T(8,128)(2,1)} collective-permute-done((bf16[2,256,192]{1,2,0:T(8,128)(2,1)}, bf16[2,256,192]{1,2,0:T(8,128)(2,1)}, u32[]{:S(2)}, u32[]{:S(2)}) %collective-permute-start.2) | collective-permute-done | bytes 196640 | tf_op jit(solution)/shard_map/ppermute | solution.py:31
  95.0 13.9 %collective-permute-done.1 = bf16[2,256,192]{1,2,0:T(8,128)(2,1)} collective-permute-done((bf16[2,256,192]{1,2,0:T(8,128)(2,1)}, bf16[2,256,192]{1,2,0:T(8,128)(2,1)}, u32[]{:S(2)}, u32[]{:S(2)}) %collective-permute-start.1) | collective-permute-done | bytes 196640 | tf_op jit(solution)/shard_map/ppermute | solution.py:31
  121.3 19.5 %while.26 = (s32[]{:T(128)}, bf16[2,1024,192]{1,2,0:T(8,128)(2,1)}, f32[2,3,1024]{2,1,0:T(4,128)}, bf16[2,1024,192]{1,2,0:T(8,128)(2,1)}, bf16[2,1024,192]{1,2,0...) while((s32[]{:T(128)}, bf16[2,1024,192]{1,2,0:T(8,128)(2,1)}, f32[2,3,1024]{2,1,0:T(4,128)}, ...), condition=%wide.region_5.6_spmd, body=%wide.region_2.5_spmd.sunk | while | flops 833811456 | bytes 48861340 | solution.py:185
  140.8 3.6 copy.84
  144.4 29.5 %all_to_all.114 = bf16[2,1024,192]{2,0,1:T(2,128)(2,1)} all-to-all(bf16[2,1024,192]{2,0,1:T(2,128)(2,1)} %copy.84), channel_id=1, replica_groups=mesh['doc'=8,'seq'=4] {'seq'}, dimensions={1} | all-to-all | bytes 1572864 | tf_op jit(solution)/shard_map/all_to_all | solution.py:188
  174.0 5.9 copy.85
  186.4 5.6 fusion.39
  194.2 2.8 multiply_reduce_fusion.2
  202.6 3.5 all-to-all-start.3
  207.9 17.4 %all-to-all-done.3 = bf16[2,256,768]{1,0,2:T(2,128)(2,1)S(1)} async-done(((bf16[2,256,768]{1,0,2:T(2,128)(2,1)}), bf16[2,256,768]{1,0,2:T(2,128)(2,1)S(1)}, u32[]{:S(2)}, u32[]{:S(2)}) %all-to-all-start.3) | async-done | bytes 786464 | tf_op jit(solution)/shard_map/all_to_all | solution.py:221
  229.3 60.3 %while.27 = (s32[]{:T(128)}, bf16[2,1024,192]{1,2,0:T(8,128)(2,1)}, bf16[2,1024,192]{1,2,0:T(8,128)(2,1)}, bf16[2,1024,192]{1,2,0:T(8,128)(2,1)}, bf16[2,1024,19...) while((s32[]{:T(128)}, bf16[2,1024,192]{1,2,0:T(8,128)(2,1)}, ...), condition=%wide.region_12.13_spmd, body=%wide.region_10.12_spmd.sunk | while | flops 2053501952 | bytes 154489168 | solution.py:223
  240.8 3.7 multiply_reduce_fusion.8
  244.5 5.3 multiply_convert_fusion.6
  249.8 4.1 convolution_bitcast_fusion.3
  270.9 3.7 multiply_reduce_fusion.8
  274.7 5.3 multiply_convert_fusion.6
  279.9 4.1 convolution_bitcast_fusion.3
  289.6 3.7 copy.93
  293.3 3.5 all-to-all-start.6
  298.9 23.1 %all-to-all-done.6 = bf16[2,1024,192]{2,0,1:T(2,128)(2,1)S(1)} async-done(((bf16[2,1024,192]{2,0,1:T(2,128)(2,1)}), bf16[2,1024,192]{2,0,1:T(2,128)(2,1)S(1)}, u32[]{:S(2)}, u32[]{:S(2)}) %all-to-all-start.6) | async-done | bytes 786464 | tf_op jit(solution)/shard_map/all_to_all | solution.py:230
  322.0 3.5 all-to-all-start.4
  327.6 23.1 %all-to-all-done.4 = bf16[2,1024,192]{2,0,1:T(2,128)(2,1)S(1)} async-done(((bf16[2,1024,192]{2,0,1:T(2,128)(2,1)}), bf16[2,1024,192]{2,0,1:T(2,128)(2,1)S(1)}, u32[]{:S(2)}, u32[]{:S(2)}) %all-to-all-start.4) | async-done | bytes 786464 | tf_op jit(solution)/shard_map/all_to_all | solution.py:228
  350.7 4.3 all-to-all-start.5
  355.3 3.6 fusion.62
  359.0 2.9 fusion.63
  363.1 5.2 fusion.40
  368.2 4.7 copy.94
  374.0 5.7 copy.90
  382.0 5.7 copy.92
  393.1 3.2 pad_maximum_fusion
  397.0 4.0 add_convert_fusion.2
  405.8 43.2 %all-reduce.2 = (f32[768]{0:T(1024)}, f32[768]{0:T(1024)}) all-reduce(f32[768]{0:T(1024)S(1)} %get-tuple-element.139, f32[768]{0:T(1024)S(1)} %copy-done.49), channel_id=1, replica_groups=mesh['doc'=8,'seq'=4] {'doc','seq'}, use_global_device_ids=true, to_apply=%region_16.17 | all-reduce | flops 1536 | bytes 12288 | tf_op jit(solution)/shard_map/psum | solution.py:260
  449.0 3.0 add_convert_fusion.1
  452.0 268.5 %all-reduce.6.cloned.1.call-done = (f32[768,2304]{0,1:T(8,128)}, f32[768,768]{1,0:T(8,128)}, f32[768,2304]{1,0:T(8,128)}, f32[1152,768]{1,0:T(8,128)}) async-done(((f32[768,2304]{0,1:T(8,128)}, f32[768,768]{1,0:T(8,128)}, f32[768,2304]{1,0:T(8,128)}, f32[1152,768]{1,0:T(8,128)}), (f32[768,2304]{0,1:T(8,128)}, f32[768,768]{1,0:T(8,128)}, f32[768,2304]{1,0:T(8,128)}, ...) | async-done | bytes 20054032 | tf_op jit(solution)/shard_map/psum | solution.py:260
  720.5 8.1 %copy.95 = f32[768,2304]{1,0:T(8,128)} copy(f32[768,2304]{0,1:T(8,128)} %get-tuple-element.177) | data formatting | bytes 14155776
  730.0 6.6 copy.143
  (244 shorter events, 135.6 us)
Async XLA Ops:
  7.2 177.1 %copy-start = (bf16[768,2304]{1,0:T(8,128)(2,1)S(1)}, bf16[768,2304]{1,0:T(8,128)(2,1)}, u32[]{:S(2)}) copy-start(bf16[768,2304]{1,0:T(8,128)(2,1)} %param.17) | copy-start | bytes 10616836
  12.8 4.3 copy-start.8
  17.1 2.2 copy-start.10
  23.3 43.9 %all-to-all-start = ((bf16[2,256,768]{1,0,2:T(2,128)(2,1)}), bf16[2,256,768]{1,0,2:T(2,128)(2,1)}, u32[]{:S(2)}, u32[]{:S(2)}) async-start(bf16[2,256,768]{1,0,2:T(2,128)(2,1)} %copy.70), calls=%async_computation | async-start | bytes 1572864 | tf_op jit(solution)/shard_map/all_to_all | solution.py:183
  33.5 8.8 %copy-start.50 = (f32[32]{0:T(128)}, f32[32]{0:T(128)S(1)}, u32[]{:S(2)}) copy-start(f32[32]{0:T(128)S(1)} %multiply_power_fusion) | copy-start | bytes 388
  67.2 50.9 %all-to-all-start.1 = ((bf16[2,256,768]{1,0,2:T(2,128)(2,1)}), bf16[2,256,768]{1,0,2:T(2,128)(2,1)}, u32[]{:S(2)}, u32[]{:S(2)}) async-start(bf16[2,256,768]{1,0,2:T(2,128)(2,1)} %copy.81), calls=%async_computation.1 | async-start | bytes 1572864 | tf_op jit(solution)/shard_map/all_to_all | solution.py:182
  76.9 18.2 %collective-permute-start.2 = (bf16[2,256,192]{1,2,0:T(8,128)(2,1)}, bf16[2,256,192]{1,2,0:T(8,128)(2,1)}, u32[]{:S(2)}, u32[]{:S(2)}) collective-permute-start(bf16[2,256,192]{1,2,0:T(8,128)(2,1)} %get-tuple-element.215), channel_id=1, source_target_pairs={{0,3},{1,2},{2,1},{3,0},{4,7},{5,6},{6,5},{7,4},{8,11},{9,10},{10,... | collective-permute-start | bytes 589832 | tf_op jit(solution)/shard_map/ppermute | solution.py:31
  80.7 28.3 %collective-permute-start.1 = (bf16[2,256,192]{1,2,0:T(8,128)(2,1)}, bf16[2,256,192]{1,2,0:T(8,128)(2,1)}, u32[]{:S(2)}, u32[]{:S(2)}) collective-permute-start(bf16[2,256,192]{1,2,0:T(8,128)(2,1)} %get-tuple-element.216), channel_id=1, source_target_pairs={{0,2},{1,3},{2,0},{3,1},{4,6},{5,7},{6,4},{7,5},{8,10},{9,11},{10,... | collective-permute-start | bytes 589832 | tf_op jit(solution)/shard_map/ppermute | solution.py:31
  80.7 28.3 %collective-permute-start = (bf16[2,256,192]{1,2,0:T(8,128)(2,1)}, bf16[2,256,192]{1,2,0:T(8,128)(2,1)}, u32[]{:S(2)}, u32[]{:S(2)}) collective-permute-start(bf16[2,256,192]{1,2,0:T(8,128)(2,1)} %get-tuple-element.217), channel_id=1, source_target_pairs={{0,1},{1,0},{2,3},{3,2},{4,5},{5,4},{6,7},{7,6},{8,9},{9,8},{10,11... | collective-permute-start | bytes 589832 | tf_op jit(solution)/shard_map/ppermute | solution.py:31
  127.5 2.7 copy-start.26
  137.2 2.7 copy-start.26
  181.2 3.0 copy-start.28
  181.2 3.1 copy-start.38
  183.9 13.2 %copy-start.6 = (f32[512,768]{1,0:T(8,128)}, f32[512,768]{1,0:T(8,128)S(1)}, u32[]{:S(2)}) copy-start(f32[512,768]{1,0:T(8,128)S(1)} %get-tuple-element.229) | copy-start | bytes 4718596
  183.9 13.2 %copy-start.41 = (f32[512]{0:T(512)}, f32[512]{0:T(512)S(1)}, u32[]{:S(2)}) copy-start(f32[512]{0:T(512)S(1)} %broadcast_multiply_fusion.3) | copy-start | bytes 6148
  184.3 12.8 %copy-start.43 = (f32[512]{0:T(512)}, f32[512]{0:T(512)S(1)}, u32[]{:S(2)}) copy-start(f32[512]{0:T(512)S(1)} %fusion.46) | copy-start | bytes 6148
  192.0 2.2 copy-start.35
  194.2 2.8 copy-start.11
  198.1 2.7 copy-start.5
  200.0 2.6 copy-start.33
  200.8 5.3 copy-start.51
  202.6 22.6 %all-to-all-start.3 = ((bf16[2,256,768]{1,0,2:T(2,128)(2,1)}), bf16[2,256,768]{1,0,2:T(2,128)(2,1)S(1)}, u32[]{:S(2)}, u32[]{:S(2)}) async-start(bf16[2,256,768]{1,0,2:T(2,128)(2,1)} %copy.86), calls=%async_computation.3 | async-start | bytes 1572864 | tf_op jit(solution)/shard_map/all_to_all | solution.py:221
  249.8 4.6 copy-start.2
  279.9 4.6 copy-start.2
  289.6 7.2 copy-start.22
  293.3 28.7 %all-to-all-start.6 = ((bf16[2,1024,192]{2,0,1:T(2,128)(2,1)}), bf16[2,1024,192]{2,0,1:T(2,128)(2,1)S(1)}, u32[]{:S(2)}, u32[]{:S(2)}) async-start(bf16[2,1024,192]{2,0,1:T(2,128)(2,1)} %copy.93), calls=%async_computation.6 | async-start | bytes 2097152 | tf_op jit(solution)/shard_map/all_to_all | solution.py:230
  296.9 28.7 %copy-start.25 = (bf16[2,1024,192]{1,2,0:T(8,128)(2,1)S(1)}, bf16[2,1024,192]{1,2,0:T(8,128)(2,1)}, u32[]{:S(2)}) copy-start(bf16[2,1024,192]{1,2,0:T(8,128)(2,1)} %get-tuple-element.103) | copy-start | bytes 2359300
  322.0 28.7 %copy-start.17 = (bf16[2,1024,192]{2,0,1:T(2,128)(2,1)}, bf16[2,1024,192]{2,0,1:T(2,128)(2,1)S(1)}, u32[]{:S(2)}) copy-start(bf16[2,1024,192]{2,0,1:T(2,128)(2,1)S(1)} %all-to-all-done.6) | copy-start | bytes 2359300
  322.0 28.7 %all-to-all-start.4 = ((bf16[2,1024,192]{2,0,1:T(2,128)(2,1)}), bf16[2,1024,192]{2,0,1:T(2,128)(2,1)S(1)}, u32[]{:S(2)}, u32[]{:S(2)}) async-start(bf16[2,1024,192]{2,0,1:T(2,128)(2,1)} %copy.89), calls=%async_computation.4 | async-start | bytes 2097152 | tf_op jit(solution)/shard_map/all_to_all | solution.py:228
  350.7 8.2 %copy-start.18 = (bf16[2,1024,192]{2,0,1:T(2,128)(2,1)}, bf16[2,1024,192]{2,0,1:T(2,128)(2,1)S(1)}, u32[]{:S(2)}) copy-start(bf16[2,1024,192]{2,0,1:T(2,128)(2,1)S(1)} %all-to-all-done.4) | copy-start | bytes 2359300
  350.7 31.2 %all-to-all-start.5 = ((bf16[2,1024,192]{2,0,1:T(2,128)(2,1)}), bf16[2,1024,192]{2,0,1:T(2,128)(2,1)}, u32[]{:S(2)}, u32[]{:S(2)}) async-start(bf16[2,1024,192]{2,0,1:T(2,128)(2,1)} %copy.91), calls=%async_computation.5 | async-start | bytes 2097152 | tf_op jit(solution)/shard_map/all_to_all | solution.py:229
  355.0 3.9 copy-start.14
  355.0 365.4 %all-reduce.6.cloned.1.call-start = ((), (), s32[]{:S(2)}) async-start(), calls=%async_computation.7 | async-start | bytes 40108032 | tf_op jit(solution)/shard_map/psum | solution.py:260
  355.2 3.7 copy-start.16
  358.9 3.0 copy-start.7
  358.9 3.0 copy-start.12
  358.9 4.1 copy-start.36
  358.9 4.1 copy-start.39
  359.0 4.1 copy-start.42
  359.0 4.1 copy-start.44
  379.7 9.3 %copy-start.9 = (bf16[2,256,768]{2,1,0:T(8,128)(2,1)S(1)}, bf16[2,256,768]{2,1,0:T(8,128)(2,1)}, u32[]{:S(2)}) copy-start(bf16[2,256,768]{2,1,0:T(8,128)(2,1)} %copy-done.8) | copy-start | bytes 2359300
  389.0 3.0 copy-start.31
  397.0 4.1 copy-start.30
  397.0 4.1 copy-start.37
  405.0 44.0 %copy-start.46 = (f32[512]{0:T(512)S(1)}, f32[512]{0:T(512)}, u32[]{:S(2)}) copy-start(f32[512]{0:T(512)} %copy-done.45) | copy-start | bytes 6148
  720.5 8.1 %copy-start.34 = (f32[768,768]{1,0:T(8,128)S(1)}, f32[768,768]{1,0:T(8,128)}, u32[]{:S(2)}) copy-start(f32[768,768]{1,0:T(8,128)} %get-tuple-element.437) | copy-start | bytes 7077892
  730.0 6.6 copy-start.19
  730.0 8.4 %copy-start.1 = (bf16[768,2304]{1,0:T(8,128)(2,1)S(1)}, bf16[768,2304]{1,0:T(8,128)(2,1)}, u32[]{:S(2)}) copy-start(bf16[768,2304]{1,0:T(8,128)(2,1)} %param.17) | copy-start | bytes 10616836
  (24 other events, 27.6 us)
Sparse Core Ops, SparseCore 0:
  396.5 323.9 all-reduce.5
